TPU v7x, 512 devices: a whole 4x4x16 slice. The times are simulated.
512 devices in a mesh: seq: 128 (over x, z_lo, y, core), head: 4 (over z_hi).
Axes of the slice: x: 4, y: 4, z: 16 (z_hi: 4, z_lo: 4; z = z_hi * 4 + z_lo), core: 2. Of those that a mesh axis runs over, the one named last changes fastest.
Arguments:
- query_rows: bfloat16 [65536, 2048], P('seq', 'head'), may hold values from -18 to 18
- key_rows: bfloat16 [65536, 2048], P('seq', 'head'), may hold values from -18 to 18
- value_rows: bfloat16 [65536, 2048], P('seq', 'head'), may hold values from -6 to 6
- out_grad: bfloat16 [65536, 4096], P('seq', 'head'), may hold values from -6 to 6
- out_weight: bfloat16 [2048, 4096], P('head', 'seq'), may hold values from -0.09375 to 0.09375
Outputs:
- attended: bfloat16 [65536, 2048], P('seq', 'head')
- query_grad: bfloat16 [65536, 2048], P('seq', 'head')
- key_grad: bfloat16 [65536, 2048], P('seq', 'head')
- value_grad: bfloat16 [65536, 2048], P('seq', 'head')
All inputs are finite; a program needn't handle non-finite values.
Results may differ from a plain program's by a relative error of at most 0.0067.
Values may be sent and summed in bfloat16 or wider, within the bound.
No kernel may reach another device: no remote copies, remote signals or barrier semaphores. Data moves between devices by JAX's collectives and lax.ppermute only.
A program may use at most 64 MiB of HBM per device.

v0:
```python
import jax
import jax.numpy as jnp
from jax import lax
from jax.sharding import PartitionSpec as P

DH = 128
BLOCK = 128
SENTINEL = -1e30


def part_forward(queries, keys_part, values_part, visible, scaling, layout_forms):
    query_form, key_form, score_form, row_order, score_order = layout_forms
    scores = (
        jnp.einsum(
            query_form + "," + key_form + "->" + score_form,
            queries,
            keys_part,
            preferred_element_type=jnp.float32,
        )
        * scaling
    )
    row_max = jnp.max(jnp.where(visible, scores, SENTINEL), axis=-1)
    weights = jnp.where(visible, jnp.exp(scores - row_max[..., None]), 0.0)
    row_sum = jnp.sum(weights, axis=-1)
    partial_out = jnp.einsum(
        score_form + "," + key_form + "->" + query_form,
        weights.astype(jnp.bfloat16),
        values_part,
        preferred_element_type=jnp.float32,
    )
    return (
        scores,
        jnp.transpose(row_max, row_order),
        jnp.transpose(row_sum, row_order),
        partial_out,
    )


def part_backward(
    scores,
    visible,
    lse_rows,
    delta_rows,
    queries,
    keys_part,
    values_part,
    grad_part,
    scaling,
    layout_forms,
):
    query_form, key_form, score_form, row_order, score_order = layout_forms
    probs = jnp.where(
        visible, jnp.exp(scores - jnp.transpose(lse_rows, score_order)[..., None]), 0.0
    )
    value_part_grad = jnp.einsum(
        score_form + "," + query_form + "->" + key_form,
        probs.astype(jnp.bfloat16),
        grad_part,
        preferred_element_type=jnp.float32,
    )
    dprob = jnp.einsum(
        query_form + "," + key_form + "->" + score_form,
        grad_part,
        values_part,
        preferred_element_type=jnp.float32,
    )
    dscore = (probs * (dprob - jnp.transpose(delta_rows, score_order)[..., None])).astype(
        jnp.bfloat16
    )
    query_part_grad = (
        jnp.einsum(
            score_form + "," + key_form + "->" + query_form,
            dscore,
            keys_part,
            preferred_element_type=jnp.float32,
        )
        * scaling
    )
    key_part_grad = (
        jnp.einsum(
            score_form + "," + query_form + "->" + key_form,
            dscore,
            queries,
            preferred_element_type=jnp.float32,
        )
        * scaling
    )
    return (query_part_grad, key_part_grad, value_part_grad)


def combine_stats(max_band, sum_band, dot_band, max_strided, sum_strided, dot_strided):
    top = jnp.maximum(max_band, max_strided)
    band_factor = jnp.exp(max_band - top)
    strided_factor = jnp.exp(max_strided - top)
    total = band_factor * sum_band + strided_factor * sum_strided
    delta = (band_factor * dot_band + strided_factor * dot_strided) / total
    return (band_factor, strided_factor, total, top + jnp.log(total), delta)


def local(query_rows, key_rows, value_rows, out_grad, out_weight):
    tokens_here, width_here = query_rows.shape
    heads_here = width_here // DH
    groups = lax.axis_size("seq")
    residues = tokens_here // groups
    blocks_here = tokens_here // BLOCK
    scaling = DH ** (-0.5)
    band_forms = ("bihd", "bjhd", "bhij", (0, 2, 1), (0, 2, 1))
    strided_forms = ("ishd", "jshd", "shij", (2, 0, 1), (1, 2, 0))
    band_rows = lax.broadcasted_iota(jnp.int32, (BLOCK, BLOCK), 0)
    band_cols = lax.broadcasted_iota(jnp.int32, (BLOCK, BLOCK), 1)
    band_visible = band_cols <= band_rows
    far_rows = lax.broadcasted_iota(jnp.int32, (groups, groups), 0)
    far_cols = lax.broadcasted_iota(jnp.int32, (groups, groups), 1)
    strided_visible = far_cols < far_rows

    def band_view(values):
        return values.reshape(blocks_here, BLOCK, heads_here, DH)

    def group_view(values):
        return values.reshape(groups, residues, width_here)

    def strided_view(values):
        return values.reshape(groups, residues, heads_here, DH)

    full_grad = lax.all_gather(out_grad, "head", axis=1, tiled=True)
    grad_rows = lax.dot_general(
        full_grad,
        lax.all_gather(out_weight, "seq", axis=1, tiled=True),
        (((1,), (1,)), ((), ())),
        preferred_element_type=jnp.float32,
    ).astype(jnp.bfloat16)
    strided_query, strided_key, strided_value, strided_grad = (
        lax.all_to_all(group_view(query_rows), "seq", split_axis=0, concat_axis=0, tiled=True),
        lax.all_to_all(group_view(key_rows), "seq", split_axis=0, concat_axis=0, tiled=True),
        lax.all_to_all(group_view(value_rows), "seq", split_axis=0, concat_axis=0, tiled=True),
        lax.all_to_all(group_view(grad_rows), "seq", split_axis=0, concat_axis=0, tiled=True),
    )
    query_band = band_view(query_rows)
    key_band = band_view(key_rows)
    value_band = band_view(value_rows)
    band_scores, max_band, sum_band, out_band = part_forward(
        query_band, key_band, value_band, band_visible, scaling, band_forms
    )
    max_band = max_band.reshape(tokens_here, heads_here)
    sum_band = sum_band.reshape(tokens_here, heads_here)
    out_band = out_band.reshape(tokens_here, heads_here, DH)
    grad_heads = grad_rows.reshape(tokens_here, heads_here, DH)
    dot_band = jnp.sum(grad_heads.astype(jnp.float32) * out_band, axis=-1)
    far_query = strided_view(strided_query)
    far_key = strided_view(strided_key)
    far_value = strided_view(strided_value)
    far_scores, max_far, sum_far, out_far = part_forward(
        far_query, far_key, far_value, strided_visible, scaling, strided_forms
    )
    max_band_split = max_band.reshape(groups, residues, heads_here)
    sum_band_split = sum_band.reshape(groups, residues, heads_here)
    dot_band_split = dot_band.reshape(groups, residues, heads_here)
    home_out, home_max, home_sum, band_max_far, band_sum_far, band_dot_far = (
        lax.all_to_all(out_far, "seq", split_axis=0, concat_axis=0, tiled=True),
        lax.all_to_all(max_far, "seq", split_axis=0, concat_axis=0, tiled=True),
        lax.all_to_all(sum_far, "seq", split_axis=0, concat_axis=0, tiled=True),
        lax.all_to_all(max_band_split, "seq", split_axis=0, concat_axis=0, tiled=True),
        lax.all_to_all(sum_band_split, "seq", split_axis=0, concat_axis=0, tiled=True),
        lax.all_to_all(dot_band_split, "seq", split_axis=0, concat_axis=0, tiled=True),
    )
    home_out = home_out.reshape(tokens_here, heads_here, DH)
    home_max = home_max.reshape(tokens_here, heads_here)
    home_sum = home_sum.reshape(tokens_here, heads_here)
    home_dot = jnp.sum(grad_heads.astype(jnp.float32) * home_out, axis=-1)
    band_factor, far_factor, total, lse_home, delta_home = combine_stats(
        max_band, sum_band, dot_band, home_max, home_sum, home_dot
    )
    attended = (
        ((band_factor[..., None] * out_band + far_factor[..., None] * home_out) / total[..., None])
        .astype(jnp.bfloat16)
        .reshape(tokens_here, width_here)
    )
    far_grad = strided_view(strided_grad)
    far_dot = jnp.sum(far_grad.astype(jnp.float32) * out_far, axis=-1)
    far_stats = combine_stats(band_max_far, band_sum_far, band_dot_far, max_far, sum_far, far_dot)
    band_grads = part_backward(
        band_scores,
        band_visible,
        lse_home.reshape(blocks_here, BLOCK, heads_here),
        delta_home.reshape(blocks_here, BLOCK, heads_here),
        query_band,
        key_band,
        value_band,
        band_view(grad_rows),
        scaling,
        band_forms,
    )
    far_grads = part_backward(
        far_scores,
        strided_visible,
        far_stats[3],
        far_stats[4],
        far_query,
        far_key,
        far_value,
        far_grad,
        scaling,
        strided_forms,
    )
    home_query, home_key, home_value = (
        lax.all_to_all(
            far_grads[0].astype(jnp.bfloat16).reshape(groups, residues, width_here),
            "seq",
            split_axis=0,
            concat_axis=0,
            tiled=True,
        ),
        lax.all_to_all(
            far_grads[1].astype(jnp.bfloat16).reshape(groups, residues, width_here),
            "seq",
            split_axis=0,
            concat_axis=0,
            tiled=True,
        ),
        lax.all_to_all(
            far_grads[2].astype(jnp.bfloat16).reshape(groups, residues, width_here),
            "seq",
            split_axis=0,
            concat_axis=0,
            tiled=True,
        ),
    )
    query_grad = (
        band_grads[0].reshape(tokens_here, width_here)
        + home_query.reshape(tokens_here, width_here).astype(jnp.float32)
    ).astype(jnp.bfloat16)
    key_grad = (
        band_grads[1].reshape(tokens_here, width_here)
        + home_key.reshape(tokens_here, width_here).astype(jnp.float32)
    ).astype(jnp.bfloat16)
    value_grad = (
        band_grads[2].reshape(tokens_here, width_here)
        + home_value.reshape(tokens_here, width_here).astype(jnp.float32)
    ).astype(jnp.bfloat16)
    return (attended, query_grad, key_grad, value_grad)


def solution(mesh):
    placed = (
        P("seq", "head"),
        P("seq", "head"),
        P("seq", "head"),
        P("seq", "head"),
        P("head", "seq"),
    )
    return jax.shard_map(
        local,
        mesh=mesh,
        in_specs=placed,
        out_specs=(P("seq", "head"), P("seq", "head"), P("seq", "head"), P("seq", "head")),
        check_vma=False,
    )
```

profile of v0, /device:TPU:1, one launch (start us, length us, event | category | flops | bytes accessed | tf_op | source)
XLA Modules:
  0.0 643.3 jit_solution(7288752029031276424)
XLA Ops:
  13.1 13.8 %all-to-all-start.7 = ((f32[128,4,4]{1,2,0:T(4,128)}), f32[128,4,4]{1,2,0:T(4,128)S(1)}, u32[]{:S(2)}, u32[]{:S(2)}) async-start(f32[128,4,4]{1,2,0:T(4,128)} %copy.166), calls=%async_computation.7 | async-start | bytes 524288 | tf_op jit(solution)/shard_map/all_to_all | solution.py:163
  27.9 1.8 copy.162
  29.8 10.4 %all-to-all-done.7 = f32[128,4,4]{1,2,0:T(4,128)S(1)} async-done(((f32[128,4,4]{1,2,0:T(4,128)}), f32[128,4,4]{1,2,0:T(4,128)S(1)}, u32[]{:S(2)}, u32[]{:S(2)}) %all-to-all-start.7) | async-done | bytes 8224 | tf_op jit(solution)/shard_map/all_to_all | solution.py:163
  40.2 6.8 %all-to-all-start.6 = ((f32[128,4,4]{1,2,0:T(4,128)}), f32[128,4,4]{1,2,0:T(4,128)}, u32[]{:S(2)}, u32[]{:S(2)}) async-start(f32[128,4,4]{1,2,0:T(4,128)} %copy.162), calls=%async_computation.6 | async-start | bytes 524288 | tf_op jit(solution)/shard_map/all_to_all | solution.py:162
  47.9 87.7 %all-to-all-done.6 = f32[128,4,4]{1,2,0:T(4,128)} async-done(((f32[128,4,4]{1,2,0:T(4,128)}), f32[128,4,4]{1,2,0:T(4,128)}, u32[]{:S(2)}, u32[]{:S(2)}) %all-to-all-start.6) | async-done | bytes 8224 | tf_op jit(solution)/shard_map/all_to_all | solution.py:162
  135.6 6.7 %all-to-all-start = ((bf16[128,4,512]{2,1,0:T(4,128)(2,1)}), bf16[128,4,512]{2,1,0:T(4,128)(2,1)S(1)}, u32[]{:S(2)}, u32[]{:S(2)}) async-start(bf16[128,4,512]{2,1,0:T(4,128)(2,1)} %reshape.175), calls=%async_computation | async-start | bytes 1048576 | tf_op jit(solution)/shard_map/all_to_all | solution.py:133
  143.2 49.3 %all-to-all-done = bf16[128,4,512]{2,1,0:T(4,128)(2,1)S(1)} async-done(((bf16[128,4,512]{2,1,0:T(4,128)(2,1)}), bf16[128,4,512]{2,1,0:T(4,128)(2,1)S(1)}, u32[]{:S(2)}, u32[]{:S(2)}) %all-to-all-start) | async-done | bytes 524320 | tf_op jit(solution)/shard_map/all_to_all | solution.py:133
  192.5 5.9 all-to-all-start.1
  199.4 17.4 %all-to-all-done.1 = bf16[128,4,512]{2,1,0:T(4,128)(2,1)S(1)} async-done(((bf16[128,4,512]{2,1,0:T(4,128)(2,1)}), bf16[128,4,512]{2,1,0:T(4,128)(2,1)S(1)}, u32[]{:S(2)}, u32[]{:S(2)}) %all-to-all-start.1) | async-done | bytes 524320 | tf_op jit(solution)/shard_map/all_to_all | solution.py:134
  216.8 8.1 %all-to-all-start.3 = ((bf16[128,4,512]{2,1,0:T(4,128)(2,1)}), bf16[128,4,512]{2,1,0:T(4,128)(2,1)}, u32[]{:S(2)}, u32[]{:S(2)}) async-start(bf16[128,4,512]{2,1,0:T(4,128)(2,1)} %reshape.182), calls=%async_computation.3 | async-start | bytes 1048576 | tf_op jit(solution)/shard_map/all_to_all | solution.py:135
  225.1 176.4 %all-gather.5.cloned.1.call-done = bf16[512,4096]{0,1:T(8,128)(2,1)} async-done(((bf16[512,32]{0,1:T(8,128)(2,1)}), bf16[512,4096]{0,1:T(8,128)(2,1)}) %all-gather.5.cloned.1.call-update) | async-done | bytes 4194320 | tf_op jit(solution)/shard_map/all_gather | solution.py:128
  401.5 5.8 convolution_convert_fusion.1
  412.1 1.8 copy.172
  413.9 8.6 %all-to-all-start.9 = ((f32[128,4,4]{1,2,0:T(4,128)}), f32[128,4,4]{1,2,0:T(4,128)}, u32[]{:S(2)}, u32[]{:S(2)}) async-start(f32[128,4,4]{1,2,0:T(4,128)} %copy.172), calls=%async_computation.9 | async-start | bytes 524288 | tf_op jit(solution)/shard_map/all_to_all | solution.py:164
  423.4 11.9 %all-to-all-done.9 = f32[128,4,4]{1,2,0:T(4,128)} async-done(((f32[128,4,4]{1,2,0:T(4,128)}), f32[128,4,4]{1,2,0:T(4,128)}, u32[]{:S(2)}, u32[]{:S(2)}) %all-to-all-start.9) | async-done | bytes 8224 | tf_op jit(solution)/shard_map/all_to_all | solution.py:164
  435.4 6.9 %all-to-all-start.8 = ((bf16[128,4,512]{2,1,0:T(4,128)(2,1)}), bf16[128,4,512]{2,1,0:T(4,128)(2,1)}, u32[]{:S(2)}, u32[]{:S(2)}) async-start(bf16[128,4,512]{2,1,0:T(4,128)(2,1)} %reshape.191), calls=%async_computation.8 | async-start | bytes 1048576 | tf_op jit(solution)/shard_map/all_to_all | solution.py:136
  445.1 1.6 select_reduce_fusion
  448.6 2.2 copy.139
  451.9 8.3 %all-to-all-done.8 = bf16[128,4,512]{2,1,0:T(4,128)(2,1)} async-done(((bf16[128,4,512]{2,1,0:T(4,128)(2,1)}), bf16[128,4,512]{2,1,0:T(4,128)(2,1)}, u32[]{:S(2)}, u32[]{:S(2)}) %all-to-all-start.8) | async-done | bytes 524320 | tf_op jit(solution)/shard_map/all_to_all | solution.py:136
  460.2 6.4 all-to-all-start.5
  466.6 1.5 copy.168
  468.1 2.3 multiply_reduce_fusion
  470.4 9.5 %all-to-all-done.5 = f32[128,4,4]{1,2,0:T(4,128)S(1)} async-done(((f32[128,4,4]{1,2,0:T(4,128)}), f32[128,4,4]{1,2,0:T(4,128)S(1)}, u32[]{:S(2)}, u32[]{:S(2)}) %all-to-all-start.5) | async-done | bytes 8224 | tf_op jit(solution)/shard_map/all_to_all | solution.py:161
  479.9 7.0 %all-to-all-start.2 = ((f32[128,4,4]{1,2,0:T(4,128)}), f32[128,4,4]{1,2,0:T(4,128)}, u32[]{:S(2)}, u32[]{:S(2)}) async-start(f32[128,4,4]{1,2,0:T(4,128)} %copy.132), calls=%async_computation.2 | async-start | bytes 524288 | tf_op jit(solution)/shard_map/all_to_all | solution.py:160
  488.2 2.2 copy.186
  490.4 9.4 %all-to-all-done.2 = f32[128,4,4]{1,2,0:T(4,128)} async-done(((f32[128,4,4]{1,2,0:T(4,128)}), f32[128,4,4]{1,2,0:T(4,128)}, u32[]{:S(2)}, u32[]{:S(2)}) %all-to-all-start.2) | async-done | bytes 8224 | tf_op jit(solution)/shard_map/all_to_all | solution.py:160
  499.9 6.9 %all-to-all-start.12 = ((bf16[128,4,512]{2,1,0:T(4,128)(2,1)}), bf16[128,4,512]{2,1,0:T(4,128)(2,1)}, u32[]{:S(2)}, u32[]{:S(2)}) async-start(bf16[128,4,512]{2,1,0:T(4,128)(2,1)} %copy.186), calls=%async_computation.12 | async-start | bytes 1048576 | tf_op jit(solution)/shard_map/all_to_all | solution.py:220
  506.7 1.5 fusion.4
  509.0 1.6 fusion.6
  511.8 12.9 %all-to-all-done.12 = bf16[128,4,512]{2,1,0:T(4,128)(2,1)} async-done(((bf16[128,4,512]{2,1,0:T(4,128)(2,1)}), bf16[128,4,512]{2,1,0:T(4,128)(2,1)}, u32[]{:S(2)}, u32[]{:S(2)}) %all-to-all-start.12) | async-done | bytes 524320 | tf_op jit(solution)/shard_map/all_to_all | solution.py:220
  524.7 7.5 %all-to-all-start.11 = ((bf16[128,4,512]{2,1,0:T(4,128)(2,1)}), bf16[128,4,512]{2,1,0:T(4,128)(2,1)}, u32[]{:S(2)}, u32[]{:S(2)}) async-start(bf16[128,4,512]{2,1,0:T(4,128)(2,1)} %copy.181), calls=%async_computation.11 | async-start | bytes 1048576 | tf_op jit(solution)/shard_map/all_to_all | solution.py:213
  532.2 1.5 fusion.7
  534.9 15.3 %all-to-all-done.11 = bf16[128,4,512]{2,1,0:T(4,128)(2,1)} async-done(((bf16[128,4,512]{2,1,0:T(4,128)(2,1)}), bf16[128,4,512]{2,1,0:T(4,128)(2,1)}, u32[]{:S(2)}, u32[]{:S(2)}) %all-to-all-start.11) | async-done | bytes 524320 | tf_op jit(solution)/shard_map/all_to_all | solution.py:213
  550.1 7.5 %all-to-all-start.10 = ((bf16[128,4,512]{2,1,0:T(4,128)(2,1)}), bf16[128,4,512]{2,1,0:T(4,128)(2,1)}, u32[]{:S(2)}, u32[]{:S(2)}) async-start(bf16[128,4,512]{2,1,0:T(4,128)(2,1)} %copy.176), calls=%async_computation.10 | async-start | bytes 1048576 | tf_op jit(solution)/shard_map/all_to_all | solution.py:206
  559.0 16.5 %all-to-all-done.10 = bf16[128,4,512]{2,1,0:T(4,128)(2,1)} async-done(((bf16[128,4,512]{2,1,0:T(4,128)(2,1)}), bf16[128,4,512]{2,1,0:T(4,128)(2,1)}, u32[]{:S(2)}, u32[]{:S(2)}) %all-to-all-start.10) | async-done | bytes 524320 | tf_op jit(solution)/shard_map/all_to_all | solution.py:206
  575.6 6.8 %all-to-all-start.4 = ((f32[128,4,4,128]{3,2,1,0:T(4,128)}), f32[128,4,4,128]{3,2,1,0:T(4,128)S(1)}, u32[]{:S(2)}, u32[]{:S(2)}) async-start(f32[128,4,4,128]{3,2,1,0:T(4,128)} %copy.141), calls=%async_computation.4 | async-start | bytes 2097152 | tf_op jit(solution)/shard_map/all_to_all | solution.py:159
  588.2 2.5 copy.137
  590.7 2.1 reshape.202
  592.8 2.2 reshape.201
  595.0 2.1 reshape.200
  597.1 14.6 %all-to-all-done.4 = f32[128,4,4,128]{3,2,1,0:T(4,128)S(1)} async-done(((f32[128,4,4,128]{3,2,1,0:T(4,128)}), f32[128,4,4,128]{3,2,1,0:T(4,128)S(1)}, u32[]{:S(2)}, u32[]{:S(2)}) %all-to-all-start.4) | async-done | bytes 1048608 | tf_op jit(solution)/shard_map/all_to_all | solution.py:159
  611.8 2.6 multiply_reduce_fusion.1
  615.5 1.5 convolution_bitcast_fusion.2
  617.4 1.5 fusion.1
  621.6 2.6 copy.179
  624.2 2.6 copy.160
  626.8 2.6 fusion.8
  629.4 2.6 fusion.9
  (111 shorter events, 41.3 us)
Async XLA Ops:
  7.2 217.9 %all-gather.3.cloned.1.call-start = ((), (), s32[]{:S(2)}) async-start(), calls=%async_computation.13 | async-start | bytes 5242880 | tf_op jit(solution)/shard_map/all_gather | solution.py:125
  7.9 39.1 %copy-start.11 = (bf16[512,512]{1,0:T(8,128)(2,1)S(1)}, bf16[512,512]{1,0:T(8,128)(2,1)}, u32[]{:S(2)}) copy-start(bf16[512,512]{1,0:T(8,128)(2,1)} %param.5) | copy-start | bytes 1572868
  7.9 393.6 %all-gather.5.cloned.1.call-start = ((), (), s32[]{:S(2)}) async-start(), calls=%async_computation.14 | async-start | bytes 4227072 | tf_op jit(solution)/shard_map/all_gather | solution.py:128
  9.8 1.4 copy-start.20
  11.2 132.0 %copy-start.18 = (bf16[4,128,4,128]{3,2,1,0:T(4,128)(2,1)}, bf16[4,128,4,128]{3,2,1,0:T(4,128)(2,1)S(1)}, u32[]{:S(2)}) copy-start(bf16[4,128,4,128]{3,2,1,0:T(4,128)(2,1)S(1)} %reshape.173) | copy-start | bytes 1572868
  11.2 131.1 %copy-start.12 = (bf16[512,512]{1,0:T(8,128)(2,1)S(1)}, bf16[512,512]{1,0:T(8,128)(2,1)}, u32[]{:S(2)}) copy-start(bf16[512,512]{1,0:T(8,128)(2,1)} %param.6) | copy-start | bytes 1572868
  11.8 186.7 %copy-start.13 = (bf16[512,512]{1,0:T(8,128)(2,1)S(1)}, bf16[512,512]{1,0:T(8,128)(2,1)}, u32[]{:S(2)}) copy-start(bf16[512,512]{1,0:T(8,128)(2,1)} %param.7) | copy-start | bytes 1572868
  13.1 27.0 %all-to-all-start.7 = ((f32[128,4,4]{1,2,0:T(4,128)}), f32[128,4,4]{1,2,0:T(4,128)S(1)}, u32[]{:S(2)}, u32[]{:S(2)}) async-start(f32[128,4,4]{1,2,0:T(4,128)} %copy.166), calls=%async_computation.7 | async-start | bytes 524288 | tf_op jit(solution)/shard_map/all_to_all | solution.py:163
  40.2 95.4 %all-to-all-start.6 = ((f32[128,4,4]{1,2,0:T(4,128)}), f32[128,4,4]{1,2,0:T(4,128)}, u32[]{:S(2)}, u32[]{:S(2)}) async-start(f32[128,4,4]{1,2,0:T(4,128)} %copy.162), calls=%async_computation.6 | async-start | bytes 524288 | tf_op jit(solution)/shard_map/all_to_all | solution.py:162
  135.6 57.0 %all-to-all-start = ((bf16[128,4,512]{2,1,0:T(4,128)(2,1)}), bf16[128,4,512]{2,1,0:T(4,128)(2,1)S(1)}, u32[]{:S(2)}, u32[]{:S(2)}) async-start(bf16[128,4,512]{2,1,0:T(4,128)(2,1)} %reshape.175), calls=%async_computation | async-start | bytes 1048576 | tf_op jit(solution)/shard_map/all_to_all | solution.py:133
  192.5 214.8 %copy-start.14 = (bf16[128,4,512]{2,1,0:T(4,128)(2,1)}, bf16[128,4,512]{2,1,0:T(4,128)(2,1)S(1)}, u32[]{:S(2)}) copy-start(bf16[128,4,512]{2,1,0:T(4,128)(2,1)S(1)} %all-to-all-done) | copy-start | bytes 1572868
  192.5 24.3 %all-to-all-start.1 = ((bf16[128,4,512]{2,1,0:T(4,128)(2,1)}), bf16[128,4,512]{2,1,0:T(4,128)(2,1)S(1)}, u32[]{:S(2)}, u32[]{:S(2)}) async-start(bf16[128,4,512]{2,1,0:T(4,128)(2,1)} %reshape.177), calls=%async_computation.1 | async-start | bytes 1048576 | tf_op jit(solution)/shard_map/all_to_all | solution.py:134
  216.8 8.3 %copy-start.16 = (bf16[128,4,512]{2,1,0:T(4,128)(2,1)}, bf16[128,4,512]{2,1,0:T(4,128)(2,1)S(1)}, u32[]{:S(2)}) copy-start(bf16[128,4,512]{2,1,0:T(4,128)(2,1)S(1)} %all-to-all-done.1) | copy-start | bytes 1572868
  216.8 197.1 %all-to-all-start.3 = ((bf16[128,4,512]{2,1,0:T(4,128)(2,1)}), bf16[128,4,512]{2,1,0:T(4,128)(2,1)}, u32[]{:S(2)}, u32[]{:S(2)}) async-start(bf16[128,4,512]{2,1,0:T(4,128)(2,1)} %reshape.182), calls=%async_computation.3 | async-start | bytes 1048576 | tf_op jit(solution)/shard_map/all_to_all | solution.py:135
  225.1 184.6 %copy-start.9 = (bf16[4,128,4,128]{3,2,1,0:T(4,128)(2,1)}, bf16[4,128,4,128]{3,2,1,0:T(4,128)(2,1)S(1)}, u32[]{:S(2)}) copy-start(bf16[4,128,4,128]{3,2,1,0:T(4,128)(2,1)S(1)} %reshape.180) | copy-start | bytes 1572868
  407.3 28.0 %copy-start = (bf16[512,512]{1,0:T(8,128)(2,1)}, bf16[512,512]{1,0:T(8,128)(2,1)S(1)}, u32[]{:S(2)}) copy-start(bf16[512,512]{1,0:T(8,128)(2,1)S(1)} %convolution_convert_fusion.1) | copy-start | bytes 1572868
  408.3 35.1 %copy-start.15 = (bf16[128,4,512]{2,1,0:T(4,128)(2,1)S(1)}, bf16[128,4,512]{2,1,0:T(4,128)(2,1)}, u32[]{:S(2)}) copy-start(bf16[128,4,512]{2,1,0:T(4,128)(2,1)} %copy-done.14) | copy-start | bytes 1572868
  411.1 33.6 %copy-start.17 = (bf16[128,4,512]{2,1,0:T(4,128)(2,1)S(1)}, bf16[128,4,512]{2,1,0:T(4,128)(2,1)}, u32[]{:S(2)}) copy-start(bf16[128,4,512]{2,1,0:T(4,128)(2,1)} %copy-done.16) | copy-start | bytes 1572868
  413.9 21.5 %all-to-all-start.9 = ((f32[128,4,4]{1,2,0:T(4,128)}), f32[128,4,4]{1,2,0:T(4,128)}, u32[]{:S(2)}, u32[]{:S(2)}) async-start(f32[128,4,4]{1,2,0:T(4,128)} %copy.172), calls=%async_computation.9 | async-start | bytes 524288 | tf_op jit(solution)/shard_map/all_to_all | solution.py:164
  435.4 24.8 %all-to-all-start.8 = ((bf16[128,4,512]{2,1,0:T(4,128)(2,1)}), bf16[128,4,512]{2,1,0:T(4,128)(2,1)}, u32[]{:S(2)}, u32[]{:S(2)}) async-start(bf16[128,4,512]{2,1,0:T(4,128)(2,1)} %reshape.191), calls=%async_computation.8 | async-start | bytes 1048576 | tf_op jit(solution)/shard_map/all_to_all | solution.py:136
  445.1 15.1 %copy-start.3 = (bf16[128,4,512]{0,2,1:T(8,128)(2,1)}, bf16[128,4,512]{0,2,1:T(8,128)(2,1)S(1)}, u32[]{:S(2)}) copy-start(bf16[128,4,512]{0,2,1:T(8,128)(2,1)S(1)} %copy.129) | copy-start | bytes 1572868
  460.2 19.7 %all-to-all-start.5 = ((f32[128,4,4]{1,2,0:T(4,128)}), f32[128,4,4]{1,2,0:T(4,128)S(1)}, u32[]{:S(2)}, u32[]{:S(2)}) async-start(f32[128,4,4]{1,2,0:T(4,128)} %copy.142), calls=%async_computation.5 | async-start | bytes 524288 | tf_op jit(solution)/shard_map/all_to_all | solution.py:161
  479.9 30.7 %copy-start.24 = (f32[128,4,4]{1,2,0:T(4,128)}, f32[128,4,4]{1,2,0:T(4,128)S(1)}, u32[]{:S(2)}) copy-start(f32[128,4,4]{1,2,0:T(4,128)S(1)} %all-to-all-done.5) | copy-start | bytes 24580
  479.9 20.0 %all-to-all-start.2 = ((f32[128,4,4]{1,2,0:T(4,128)}), f32[128,4,4]{1,2,0:T(4,128)}, u32[]{:S(2)}, u32[]{:S(2)}) async-start(f32[128,4,4]{1,2,0:T(4,128)} %copy.132), calls=%async_computation.2 | async-start | bytes 524288 | tf_op jit(solution)/shard_map/all_to_all | solution.py:160
  499.9 24.8 %all-to-all-start.12 = ((bf16[128,4,512]{2,1,0:T(4,128)(2,1)}), bf16[128,4,512]{2,1,0:T(4,128)(2,1)}, u32[]{:S(2)}, u32[]{:S(2)}) async-start(bf16[128,4,512]{2,1,0:T(4,128)(2,1)} %copy.186), calls=%async_computation.12 | async-start | bytes 1048576 | tf_op jit(solution)/shard_map/all_to_all | solution.py:220
  508.2 0.8 copy-start.2
  509.0 48.6 %copy-start.4 = (f32[128,4,4,128]{0,3,2,1:T(8,128)S(1)}, f32[128,4,4,128]{0,3,2,1:T(8,128)}, u32[]{:S(2)}) copy-start(f32[128,4,4,128]{0,3,2,1:T(8,128)} %get-tuple-element.16) | copy-start | bytes 3145732
  524.7 25.4 %all-to-all-start.11 = ((bf16[128,4,512]{2,1,0:T(4,128)(2,1)}), bf16[128,4,512]{2,1,0:T(4,128)(2,1)}, u32[]{:S(2)}, u32[]{:S(2)}) async-start(bf16[128,4,512]{2,1,0:T(4,128)(2,1)} %copy.181), calls=%async_computation.11 | async-start | bytes 1048576 | tf_op jit(solution)/shard_map/all_to_all | solution.py:213
  534.9 52.0 %copy-start.1 = (bf16[512,512]{1,0:T(8,128)(2,1)S(1)}, bf16[512,512]{1,0:T(8,128)(2,1)}, u32[]{:S(2)}) copy-start(bf16[512,512]{1,0:T(8,128)(2,1)} %copy-done) | copy-start | bytes 1572868
  550.1 25.4 %all-to-all-start.10 = ((bf16[128,4,512]{2,1,0:T(4,128)(2,1)}), bf16[128,4,512]{2,1,0:T(4,128)(2,1)}, u32[]{:S(2)}, u32[]{:S(2)}) async-start(bf16[128,4,512]{2,1,0:T(4,128)(2,1)} %copy.176), calls=%async_computation.10 | async-start | bytes 1048576 | tf_op jit(solution)/shard_map/all_to_all | solution.py:206
  575.6 36.2 %all-to-all-start.4 = ((f32[128,4,4,128]{3,2,1,0:T(4,128)}), f32[128,4,4,128]{3,2,1,0:T(4,128)S(1)}, u32[]{:S(2)}, u32[]{:S(2)}) async-start(f32[128,4,4,128]{3,2,1,0:T(4,128)} %copy.141), calls=%async_computation.4 | async-start | bytes 2097152 | tf_op jit(solution)/shard_map/all_to_all | solution.py:159
  592.8 24.1 %copy-start.10 = (bf16[4,128,4,128]{3,2,1,0:T(4,128)(2,1)S(1)}, bf16[4,128,4,128]{3,2,1,0:T(4,128)(2,1)}, u32[]{:S(2)}) copy-start(bf16[4,128,4,128]{3,2,1,0:T(4,128)(2,1)} %copy-done.9) | copy-start | bytes 1572868
  615.4 1.9 copy-start.21
  615.4 3.5 copy-start.19
  617.4 2.9 copy-start.6
  624.2 7.8 %copy-start.5 = (f32[512,512]{1,0:T(8,128)S(1)}, f32[512,512]{1,0:T(8,128)}, u32[]{:S(2)}) copy-start(f32[512,512]{1,0:T(8,128)} %reshape.200) | copy-start | bytes 3145732
  626.8 5.2 copy-start.7
  626.8 6.8 %copy-start.22 = (f32[512,4]{1,0:T(8,128)S(1)}, f32[512,4]{1,0:T(8,128)}, u32[]{:S(2)}) copy-start(f32[512,4]{1,0:T(8,128)} %copy.138) | copy-start | bytes 24580
  629.4 4.8 copy-start.23
  629.4 5.4 copy-start.8
Sparse Core Ops, SparseCore 0:
  10.1 123.5 all-gather.2
  135.8 265.6 all-gather.4
where the time goes:
time: 653 us; the launch traced here: 643 us
  waiting for transfers between devices  441 us (68%)
  starting transfers between devices  98.9 us (15%)
  local copies, waits for them, and re-layouts  55.7 us (9%)
  matrix products  22.2 us (3%)
  between operations  14.7 us (2%)
  other arithmetic  10.7 us (2%)
    all_gather x1, waiting for transfers between devices, local(): lax.all_gather(out_weight, 'seq', axis=1, tiled=True)  176 us
    all_to_all x1, waiting for transfers between devices, local(): lax.all_to_all(max_band_split, 'seq', split_axis=0, concat_axis=0, tiled=...  87.7 us
    all_to_all x1, waiting for transfers between devices, local(): lax.all_to_all(group_view(query_rows), 'seq', split_axis=0, concat_axis=0...  49.3 us
    all_to_all x1, waiting for transfers between devices, local(): lax.all_to_all(group_view(key_rows), 'seq', split_axis=0, concat_axis=0,...  17.4 us
    all_to_all x1, waiting for transfers between devices, local(): lax.all_to_all(far_grads[0].astype(jnp.bfloat16).reshape(groups, residues...  16.5 us
    all_to_all x1, waiting for transfers between devices, local(): lax.all_to_all(far_grads[1].astype(jnp.bfloat16).reshape(groups, residues...  15.3 us
    all_to_all x1, waiting for transfers between devices, local(): lax.all_to_all(out_far, 'seq', split_axis=0, concat_axis=0, tiled=True)  14.6 us
    all_to_all x1, starting transfers between devices, local(): lax.all_to_all(sum_band_split, 'seq', split_axis=0, concat_axis=0, tiled=...  13.8 us
  transfers between devices with their start and end apart: 15, of which 13 were waited for; matrix products, arithmetic and copies ran while one was open for 10% of the time, Pallas kernels for 0%

commit v1 on v0

--- a/solution.py
+++ b/solution.py
@@ -1,3 +1,4 @@
+import functools
 import jax
 import jax.numpy as jnp
 from jax import lax
@@ -6,6 +7,16 @@
 DH = 128
 BLOCK = 128
 SENTINEL = -1e30
+
+
+def report_chunk(unit, named_axis):
+    return jnp.concatenate(
+        lax.all_to_all(jnp.stack(lax.axis_size(named_axis) * [unit], axis=0), named_axis, 0, 0),
+        axis=1,
+    )
+
+
+push_columns = functools.partial(report_chunk, named_axis="seq")
 
 
 def part_forward(queries, keys_part, values_part, visible, scaling, layout_forms):
@@ -125,7 +136,7 @@
     full_grad = lax.all_gather(out_grad, "head", axis=1, tiled=True)
     grad_rows = lax.dot_general(
         full_grad,
-        lax.all_gather(out_weight, "seq", axis=1, tiled=True),
+        push_columns(out_weight),
         (((1,), (1,)), ((), ())),
         preferred_element_type=jnp.float32,
     ).astype(jnp.bfloat16)

time: 653 us -> 613 us (0.939)
  waiting for transfers between devices: 441 us -> 375 us
  blocking collectives: 0 us -> 24.8 us
    all_to_all x1, waiting for transfers between devices: 17.4 us -> 230 us  [report_chunk(): lax.all_to_all(jnp.stack(lax.axis_size(named_axis) * [unit], axis=0), nam...]
    all_gather x1 -> x0, waiting for transfers between devices: 176 us -> none  [local(): lax.all_gather(out_weight, 'seq', axis=1, tiled=True)]
    all_to_all x1, waiting for transfers between devices: 87.7 us -> 11.9 us  [local(): lax.all_to_all(max_band_split, 'seq', split_axis=0, concat_axis=0, tiled=...]
    all_to_all x1, waiting for transfers between devices: 49.3 us -> 18.1 us  [local(): lax.all_to_all(group_view(query_rows), 'seq', split_axis=0, concat_axis=0...]
    all_to_all x0 -> x1, blocking collectives: none -> 24.8 us  [local(): lax.all_to_all(group_view(key_rows), 'seq', split_axis=0, concat_axis=0,...]
  transfers between devices with their start and end apart: 15 -> 14, of which waited for: 13 -> 13; matrix products, arithmetic and copies ran while one was open for 10% -> 10% of each run, Pallas kernels for 0% -> 0%
where the time goes in v1:
time: 613 us; the launch traced here: 603 us
  waiting for transfers between devices  375 us (61%)
  starting transfers between devices  98.5 us (16%)
  local copies, waits for them, and re-layouts  57.4 us (9%)
  blocking collectives  24.8 us (4%)
  matrix products  22.3 us (4%)
  between operations  14.7 us (2%)
  other arithmetic  10.7 us (2%)
    all_to_all x1, waiting for transfers between devices, report_chunk(): lax.all_to_all(jnp.stack(lax.axis_size(named_axis) * [unit], axis=0), nam...  230 us
    all_to_all x1, blocking collectives, local(): lax.all_to_all(group_view(key_rows), 'seq', split_axis=0, concat_axis=0,...  24.8 us
    all_to_all x1, waiting for transfers between devices, local(): lax.all_to_all(group_view(query_rows), 'seq', split_axis=0, concat_axis=0...  18.1 us
    all_to_all x1, waiting for transfers between devices, local(): lax.all_to_all(far_grads[0].astype(jnp.bfloat16).reshape(groups, residues...  16.5 us
    all_to_all x1, waiting for transfers between devices, local(): lax.all_to_all(far_grads[1].astype(jnp.bfloat16).reshape(groups, residues...  15.3 us
    all_to_all x1, waiting for transfers between devices, local(): lax.all_to_all(out_far, 'seq', split_axis=0, concat_axis=0, tiled=True)  14.8 us
    all_to_all x1, starting transfers between devices, local(): lax.all_to_all(sum_band_split, 'seq', split_axis=0, concat_axis=0, tiled=...  13.8 us
    all_to_all x1, waiting for transfers between devices, local(): lax.all_to_all(far_grads[2].astype(jnp.bfloat16).reshape(groups, residues...  12.9 us
  transfers between devices with their start and end apart: 14, of which 13 were waited for; matrix products, arithmetic and copies ran while one was open for 10% of the time, Pallas kernels for 0%

profile of v1, /device:TPU:1, one launch (start us, length us, event | category | flops | bytes accessed | tf_op | source)
XLA Modules:
  0.0 603.3 jit_solution(8393834832992606452)
XLA Ops:
  11.7 13.8 %all-to-all-start.8 = ((f32[128,4,4]{1,2,0:T(4,128)}), f32[128,4,4]{1,2,0:T(4,128)S(1)}, u32[]{:S(2)}, u32[]{:S(2)}) async-start(f32[128,4,4]{1,2,0:T(4,128)} %copy.167), calls=%async_computation.8 | async-start | bytes 524288 | tf_op jit(solution)/shard_map/all_to_all | solution.py:174
  26.5 1.8 copy.163
  28.3 10.4 %all-to-all-done.8 = f32[128,4,4]{1,2,0:T(4,128)S(1)} async-done(((f32[128,4,4]{1,2,0:T(4,128)}), f32[128,4,4]{1,2,0:T(4,128)S(1)}, u32[]{:S(2)}, u32[]{:S(2)}) %all-to-all-start.8) | async-done | bytes 8224 | tf_op jit(solution)/shard_map/all_to_all | solution.py:174
  38.7 6.9 %all-to-all-start.7 = ((f32[128,4,4]{1,2,0:T(4,128)}), f32[128,4,4]{1,2,0:T(4,128)}, u32[]{:S(2)}, u32[]{:S(2)}) async-start(f32[128,4,4]{1,2,0:T(4,128)} %copy.163), calls=%async_computation.7 | async-start | bytes 524288 | tf_op jit(solution)/shard_map/all_to_all | solution.py:173
  46.5 11.9 %all-to-all-done.7 = f32[128,4,4]{1,2,0:T(4,128)} async-done(((f32[128,4,4]{1,2,0:T(4,128)}), f32[128,4,4]{1,2,0:T(4,128)}, u32[]{:S(2)}, u32[]{:S(2)}) %all-to-all-start.7) | async-done | bytes 8224 | tf_op jit(solution)/shard_map/all_to_all | solution.py:173
  58.4 6.0 all-to-all-start
  64.6 18.1 %all-to-all-done = bf16[128,4,512]{2,1,0:T(4,128)(2,1)S(1)} async-done(((bf16[128,4,512]{2,1,0:T(4,128)(2,1)}), bf16[128,4,512]{2,1,0:T(4,128)(2,1)S(1)}, u32[]{:S(2)}, u32[]{:S(2)}) %all-to-all-start) | async-done | bytes 524320 | tf_op jit(solution)/shard_map/all_to_all | solution.py:144
  82.6 24.8 %all_to_all.70 = bf16[128,4,512]{2,1,0:T(4,128)(2,1)} all-to-all(bf16[128,4,512]{2,1,0:T(4,128)(2,1)S(1)} %reshape.185), channel_id=1, replica_groups=mesh['seq'=128,'head'=4] {'seq'}, dimensions={0} | all-to-all | bytes 1048576 | tf_op jit(solution)/shard_map/all_to_all | solution.py:145
  107.4 2.5 stack.2
  109.9 8.2 %all-to-all-start.6 = ((bf16[128,512,32]{1,2,0:T(8,128)(2,1)}), bf16[128,512,32]{1,2,0:T(8,128)(2,1)}, u32[]{:S(2)}, u32[]{:S(2)}) async-start(bf16[128,512,32]{1,2,0:T(8,128)(2,1)} %stack.2), calls=%async_computation.6 | async-start | bytes 8388608 | tf_op jit(solution)/shard_map/all_to_all | solution.py:14
  119.7 229.8 %all-to-all-done.6 = bf16[128,512,32]{1,2,0:T(8,128)(2,1)} async-done(((bf16[128,512,32]{1,2,0:T(8,128)(2,1)}), bf16[128,512,32]{1,2,0:T(8,128)(2,1)}, u32[]{:S(2)}, u32[]{:S(2)}) %all-to-all-start.6) | async-done | bytes 4194336 | tf_op jit(solution)/shard_map/all_to_all | solution.py:14
  349.5 7.5 %all-to-all-start.3 = ((bf16[128,4,512]{2,1,0:T(4,128)(2,1)}), bf16[128,4,512]{2,1,0:T(4,128)(2,1)}, u32[]{:S(2)}, u32[]{:S(2)}) async-start(bf16[128,4,512]{2,1,0:T(4,128)(2,1)} %reshape.190), calls=%async_computation.3 | async-start | bytes 1048576 | tf_op jit(solution)/shard_map/all_to_all | solution.py:146
  357.2 5.9 convolution_convert_fusion.1
  367.8 1.8 copy.173
  369.6 5.4 all-to-all-done.3
  374.9 7.5 %all-to-all-start.10 = ((f32[128,4,4]{1,2,0:T(4,128)}), f32[128,4,4]{1,2,0:T(4,128)}, u32[]{:S(2)}, u32[]{:S(2)}) async-start(f32[128,4,4]{1,2,0:T(4,128)} %copy.173), calls=%async_computation.10 | async-start | bytes 524288 | tf_op jit(solution)/shard_map/all_to_all | solution.py:175
  383.3 12.0 %all-to-all-done.10 = f32[128,4,4]{1,2,0:T(4,128)} async-done(((f32[128,4,4]{1,2,0:T(4,128)}), f32[128,4,4]{1,2,0:T(4,128)}, u32[]{:S(2)}, u32[]{:S(2)}) %all-to-all-start.10) | async-done | bytes 8224 | tf_op jit(solution)/shard_map/all_to_all | solution.py:175
  395.4 6.9 %all-to-all-start.9 = ((bf16[128,4,512]{2,1,0:T(4,128)(2,1)}), bf16[128,4,512]{2,1,0:T(4,128)(2,1)}, u32[]{:S(2)}, u32[]{:S(2)}) async-start(bf16[128,4,512]{2,1,0:T(4,128)(2,1)} %reshape.201), calls=%async_computation.9 | async-start | bytes 1048576 | tf_op jit(solution)/shard_map/all_to_all | solution.py:147
  405.1 1.6 select_reduce_fusion
  408.6 2.2 copy.140
  411.9 8.3 %all-to-all-done.9 = bf16[128,4,512]{2,1,0:T(4,128)(2,1)} async-done(((bf16[128,4,512]{2,1,0:T(4,128)(2,1)}), bf16[128,4,512]{2,1,0:T(4,128)(2,1)}, u32[]{:S(2)}, u32[]{:S(2)}) %all-to-all-start.9) | async-done | bytes 524320 | tf_op jit(solution)/shard_map/all_to_all | solution.py:147
  420.2 6.5 %all-to-all-start.5 = ((f32[128,4,4]{1,2,0:T(4,128)}), f32[128,4,4]{1,2,0:T(4,128)S(1)}, u32[]{:S(2)}, u32[]{:S(2)}) async-start(f32[128,4,4]{1,2,0:T(4,128)} %copy.143), calls=%async_computation.5 | async-start | bytes 524288 | tf_op jit(solution)/shard_map/all_to_all | solution.py:172
  428.2 2.3 multiply_reduce_fusion
  430.5 9.5 %all-to-all-done.5 = f32[128,4,4]{1,2,0:T(4,128)S(1)} async-done(((f32[128,4,4]{1,2,0:T(4,128)}), f32[128,4,4]{1,2,0:T(4,128)S(1)}, u32[]{:S(2)}, u32[]{:S(2)}) %all-to-all-start.5) | async-done | bytes 8224 | tf_op jit(solution)/shard_map/all_to_all | solution.py:172
  440.0 6.9 %all-to-all-start.2 = ((f32[128,4,4]{1,2,0:T(4,128)}), f32[128,4,4]{1,2,0:T(4,128)}, u32[]{:S(2)}, u32[]{:S(2)}) async-start(f32[128,4,4]{1,2,0:T(4,128)} %copy.133), calls=%async_computation.2 | async-start | bytes 524288 | tf_op jit(solution)/shard_map/all_to_all | solution.py:171
  448.2 2.2 copy.187
  450.4 9.4 %all-to-all-done.2 = f32[128,4,4]{1,2,0:T(4,128)} async-done(((f32[128,4,4]{1,2,0:T(4,128)}), f32[128,4,4]{1,2,0:T(4,128)}, u32[]{:S(2)}, u32[]{:S(2)}) %all-to-all-start.2) | async-done | bytes 8224 | tf_op jit(solution)/shard_map/all_to_all | solution.py:171
  459.9 6.8 %all-to-all-start.13 = ((bf16[128,4,512]{2,1,0:T(4,128)(2,1)}), bf16[128,4,512]{2,1,0:T(4,128)(2,1)}, u32[]{:S(2)}, u32[]{:S(2)}) async-start(bf16[128,4,512]{2,1,0:T(4,128)(2,1)} %copy.187), calls=%async_computation.13 | async-start | bytes 1048576 | tf_op jit(solution)/shard_map/all_to_all | solution.py:231
  469.0 1.6 fusion.6
  471.8 12.9 %all-to-all-done.13 = bf16[128,4,512]{2,1,0:T(4,128)(2,1)} async-done(((bf16[128,4,512]{2,1,0:T(4,128)(2,1)}), bf16[128,4,512]{2,1,0:T(4,128)(2,1)}, u32[]{:S(2)}, u32[]{:S(2)}) %all-to-all-start.13) | async-done | bytes 524320 | tf_op jit(solution)/shard_map/all_to_all | solution.py:231
  484.7 7.5 %all-to-all-start.12 = ((bf16[128,4,512]{2,1,0:T(4,128)(2,1)}), bf16[128,4,512]{2,1,0:T(4,128)(2,1)}, u32[]{:S(2)}, u32[]{:S(2)}) async-start(bf16[128,4,512]{2,1,0:T(4,128)(2,1)} %copy.182), calls=%async_computation.12 | async-start | bytes 1048576 | tf_op jit(solution)/shard_map/all_to_all | solution.py:224
  492.1 1.5 fusion.7
  494.8 15.3 %all-to-all-done.12 = bf16[128,4,512]{2,1,0:T(4,128)(2,1)} async-done(((bf16[128,4,512]{2,1,0:T(4,128)(2,1)}), bf16[128,4,512]{2,1,0:T(4,128)(2,1)}, u32[]{:S(2)}, u32[]{:S(2)}) %all-to-all-start.12) | async-done | bytes 524320 | tf_op jit(solution)/shard_map/all_to_all | solution.py:224
  510.1 7.7 %all-to-all-start.11 = ((bf16[128,4,512]{2,1,0:T(4,128)(2,1)}), bf16[128,4,512]{2,1,0:T(4,128)(2,1)}, u32[]{:S(2)}, u32[]{:S(2)}) async-start(bf16[128,4,512]{2,1,0:T(4,128)(2,1)} %copy.177), calls=%async_computation.11 | async-start | bytes 1048576 | tf_op jit(solution)/shard_map/all_to_all | solution.py:217
  519.2 16.5 %all-to-all-done.11 = bf16[128,4,512]{2,1,0:T(4,128)(2,1)} async-done(((bf16[128,4,512]{2,1,0:T(4,128)(2,1)}), bf16[128,4,512]{2,1,0:T(4,128)(2,1)}, u32[]{:S(2)}, u32[]{:S(2)}) %all-to-all-start.11) | async-done | bytes 524320 | tf_op jit(solution)/shard_map/all_to_all | solution.py:217
  535.8 6.4 %all-to-all-start.4 = ((f32[128,4,4,128]{3,2,1,0:T(4,128)}), f32[128,4,4,128]{3,2,1,0:T(4,128)S(1)}, u32[]{:S(2)}, u32[]{:S(2)}) async-start(f32[128,4,4,128]{3,2,1,0:T(4,128)} %copy.142), calls=%async_computation.4 | async-start | bytes 2097152 | tf_op jit(solution)/shard_map/all_to_all | solution.py:170
  548.0 2.5 copy.138
  550.6 2.1 reshape.212
  552.7 2.2 reshape.211
  554.8 2.1 reshape.210
  556.9 14.8 %all-to-all-done.4 = f32[128,4,4,128]{3,2,1,0:T(4,128)S(1)} async-done(((f32[128,4,4,128]{3,2,1,0:T(4,128)}), f32[128,4,4,128]{3,2,1,0:T(4,128)S(1)}, u32[]{:S(2)}, u32[]{:S(2)}) %all-to-all-start.4) | async-done | bytes 1048608 | tf_op jit(solution)/shard_map/all_to_all | solution.py:170
  571.7 2.6 multiply_reduce_fusion.1
  575.5 1.5 convolution_bitcast_fusion.2
  577.3 1.5 fusion.1
  581.6 2.6 copy.180
  584.2 2.7 copy.161
  586.8 2.6 fusion.8
  589.4 2.6 fusion.9
  (106 shorter events, 42.6 us)
Async XLA Ops:
  7.2 38.4 %copy-start.11 = (bf16[512,512]{1,0:T(8,128)(2,1)S(1)}, bf16[512,512]{1,0:T(8,128)(2,1)}, u32[]{:S(2)}) copy-start(bf16[512,512]{1,0:T(8,128)(2,1)} %param.5) | copy-start | bytes 1572868
  8.4 50.0 %copy-start.17 = (bf16[4,128,4,128]{3,2,1,0:T(4,128)(2,1)}, bf16[4,128,4,128]{3,2,1,0:T(4,128)(2,1)S(1)}, u32[]{:S(2)}) copy-start(bf16[4,128,4,128]{3,2,1,0:T(4,128)(2,1)S(1)} %reshape.180) | copy-start | bytes 1572868
  9.8 54.8 %copy-start.15 = (bf16[4,128,4,128]{3,2,1,0:T(4,128)(2,1)}, bf16[4,128,4,128]{3,2,1,0:T(4,128)(2,1)S(1)}, u32[]{:S(2)}) copy-start(bf16[4,128,4,128]{3,2,1,0:T(4,128)(2,1)S(1)} %reshape.181) | copy-start | bytes 1572868
  9.8 54.6 %copy-start.12 = (bf16[512,512]{1,0:T(8,128)(2,1)S(1)}, bf16[512,512]{1,0:T(8,128)(2,1)}, u32[]{:S(2)}) copy-start(bf16[512,512]{1,0:T(8,128)(2,1)} %param.6) | copy-start | bytes 1572868
  10.3 97.1 %copy-start.22 = (bf16[512,32]{0,1:T(8,128)(2,1)S(1)}, bf16[512,32]{0,1:T(8,128)(2,1)}, u32[]{:S(2)}) copy-start(bf16[512,32]{0,1:T(8,128)(2,1)} %param.9) | copy-start | bytes 98308
  11.7 27.0 %all-to-all-start.8 = ((f32[128,4,4]{1,2,0:T(4,128)}), f32[128,4,4]{1,2,0:T(4,128)S(1)}, u32[]{:S(2)}, u32[]{:S(2)}) async-start(f32[128,4,4]{1,2,0:T(4,128)} %copy.167), calls=%async_computation.8 | async-start | bytes 524288 | tf_op jit(solution)/shard_map/all_to_all | solution.py:174
  38.7 19.7 %all-to-all-start.7 = ((f32[128,4,4]{1,2,0:T(4,128)}), f32[128,4,4]{1,2,0:T(4,128)}, u32[]{:S(2)}, u32[]{:S(2)}) async-start(f32[128,4,4]{1,2,0:T(4,128)} %copy.163), calls=%async_computation.7 | async-start | bytes 524288 | tf_op jit(solution)/shard_map/all_to_all | solution.py:173
  58.4 24.2 %all-to-all-start = ((bf16[128,4,512]{2,1,0:T(4,128)(2,1)}), bf16[128,4,512]{2,1,0:T(4,128)(2,1)S(1)}, u32[]{:S(2)}, u32[]{:S(2)}) async-start(bf16[128,4,512]{2,1,0:T(4,128)(2,1)} %reshape.183), calls=%async_computation | async-start | bytes 1048576 | tf_op jit(solution)/shard_map/all_to_all | solution.py:144
  109.9 8.9 %copy-start.13 = (bf16[512,512]{1,0:T(8,128)(2,1)S(1)}, bf16[512,512]{1,0:T(8,128)(2,1)}, u32[]{:S(2)}) copy-start(bf16[512,512]{1,0:T(8,128)(2,1)} %param.7) | copy-start | bytes 1572868
  109.9 239.6 %all-to-all-start.6 = ((bf16[128,512,32]{1,2,0:T(8,128)(2,1)}), bf16[128,512,32]{1,2,0:T(8,128)(2,1)}, u32[]{:S(2)}, u32[]{:S(2)}) async-start(bf16[128,512,32]{1,2,0:T(8,128)(2,1)} %stack.2), calls=%async_computation.6 | async-start | bytes 8388608 | tf_op jit(solution)/shard_map/all_to_all | solution.py:14
  118.1 239.1 %all-gather.2.cloned.1.call-start = ((), (), s32[]{:S(2)}) async-start(), calls=%async_computation.14 | async-start | bytes 5242880 | tf_op jit(solution)/shard_map/all_gather | solution.py:136
  349.5 25.5 %all-to-all-start.3 = ((bf16[128,4,512]{2,1,0:T(4,128)(2,1)}), bf16[128,4,512]{2,1,0:T(4,128)(2,1)}, u32[]{:S(2)}, u32[]{:S(2)}) async-start(bf16[128,4,512]{2,1,0:T(4,128)(2,1)} %reshape.190), calls=%async_computation.3 | async-start | bytes 1048576 | tf_op jit(solution)/shard_map/all_to_all | solution.py:146
  357.1 8.3 %copy-start.9 = (bf16[4,128,4,128]{3,2,1,0:T(4,128)(2,1)}, bf16[4,128,4,128]{3,2,1,0:T(4,128)(2,1)S(1)}, u32[]{:S(2)}) copy-start(bf16[4,128,4,128]{3,2,1,0:T(4,128)(2,1)S(1)} %reshape.188) | copy-start | bytes 1572868
  363.1 32.3 %copy-start = (bf16[512,512]{1,0:T(8,128)(2,1)}, bf16[512,512]{1,0:T(8,128)(2,1)S(1)}, u32[]{:S(2)}) copy-start(bf16[512,512]{1,0:T(8,128)(2,1)S(1)} %convolution_convert_fusion.1) | copy-start | bytes 1572868
  366.8 37.9 %copy-start.14 = (bf16[128,4,512]{2,1,0:T(4,128)(2,1)S(1)}, bf16[128,4,512]{2,1,0:T(4,128)(2,1)}, u32[]{:S(2)}) copy-start(bf16[128,4,512]{2,1,0:T(4,128)(2,1)} %all_to_all.70) | copy-start | bytes 1572868
  374.9 20.4 %all-to-all-start.10 = ((f32[128,4,4]{1,2,0:T(4,128)}), f32[128,4,4]{1,2,0:T(4,128)}, u32[]{:S(2)}, u32[]{:S(2)}) async-start(f32[128,4,4]{1,2,0:T(4,128)} %copy.173), calls=%async_computation.10 | async-start | bytes 524288 | tf_op jit(solution)/shard_map/all_to_all | solution.py:175
  395.4 24.8 %all-to-all-start.9 = ((bf16[128,4,512]{2,1,0:T(4,128)(2,1)}), bf16[128,4,512]{2,1,0:T(4,128)(2,1)}, u32[]{:S(2)}, u32[]{:S(2)}) async-start(bf16[128,4,512]{2,1,0:T(4,128)(2,1)} %reshape.201), calls=%async_computation.9 | async-start | bytes 1048576 | tf_op jit(solution)/shard_map/all_to_all | solution.py:147
  405.1 15.1 %copy-start.3 = (bf16[128,4,512]{0,2,1:T(8,128)(2,1)}, bf16[128,4,512]{0,2,1:T(8,128)(2,1)S(1)}, u32[]{:S(2)}) copy-start(bf16[128,4,512]{0,2,1:T(8,128)(2,1)S(1)} %copy.130) | copy-start | bytes 1572868
  420.2 19.8 %all-to-all-start.5 = ((f32[128,4,4]{1,2,0:T(4,128)}), f32[128,4,4]{1,2,0:T(4,128)S(1)}, u32[]{:S(2)}, u32[]{:S(2)}) async-start(f32[128,4,4]{1,2,0:T(4,128)} %copy.143), calls=%async_computation.5 | async-start | bytes 524288 | tf_op jit(solution)/shard_map/all_to_all | solution.py:172
  440.0 30.6 %copy-start.21 = (f32[128,4,4]{1,2,0:T(4,128)}, f32[128,4,4]{1,2,0:T(4,128)S(1)}, u32[]{:S(2)}) copy-start(f32[128,4,4]{1,2,0:T(4,128)S(1)} %all-to-all-done.5) | copy-start | bytes 24580
  440.0 19.8 %all-to-all-start.2 = ((f32[128,4,4]{1,2,0:T(4,128)}), f32[128,4,4]{1,2,0:T(4,128)}, u32[]{:S(2)}, u32[]{:S(2)}) async-start(f32[128,4,4]{1,2,0:T(4,128)} %copy.133), calls=%async_computation.2 | async-start | bytes 524288 | tf_op jit(solution)/shard_map/all_to_all | solution.py:171
  459.9 24.8 %all-to-all-start.13 = ((bf16[128,4,512]{2,1,0:T(4,128)(2,1)}), bf16[128,4,512]{2,1,0:T(4,128)(2,1)}, u32[]{:S(2)}, u32[]{:S(2)}) async-start(bf16[128,4,512]{2,1,0:T(4,128)(2,1)} %copy.187), calls=%async_computation.13 | async-start | bytes 1048576 | tf_op jit(solution)/shard_map/all_to_all | solution.py:231
  468.2 0.8 copy-start.2
  469.0 48.8 %copy-start.4 = (f32[128,4,4,128]{0,3,2,1:T(8,128)S(1)}, f32[128,4,4,128]{0,3,2,1:T(8,128)}, u32[]{:S(2)}) copy-start(f32[128,4,4,128]{0,3,2,1:T(8,128)} %get-tuple-element.16) | copy-start | bytes 3145732
  484.7 25.4 %all-to-all-start.12 = ((bf16[128,4,512]{2,1,0:T(4,128)(2,1)}), bf16[128,4,512]{2,1,0:T(4,128)(2,1)}, u32[]{:S(2)}, u32[]{:S(2)}) async-start(bf16[128,4,512]{2,1,0:T(4,128)(2,1)} %copy.182), calls=%async_computation.12 | async-start | bytes 1048576 | tf_op jit(solution)/shard_map/all_to_all | solution.py:224
  494.8 51.9 %copy-start.1 = (bf16[512,512]{1,0:T(8,128)(2,1)S(1)}, bf16[512,512]{1,0:T(8,128)(2,1)}, u32[]{:S(2)}) copy-start(bf16[512,512]{1,0:T(8,128)(2,1)} %copy-done) | copy-start | bytes 1572868
  510.1 25.6 %all-to-all-start.11 = ((bf16[128,4,512]{2,1,0:T(4,128)(2,1)}), bf16[128,4,512]{2,1,0:T(4,128)(2,1)}, u32[]{:S(2)}, u32[]{:S(2)}) async-start(bf16[128,4,512]{2,1,0:T(4,128)(2,1)} %copy.177), calls=%async_computation.11 | async-start | bytes 1048576 | tf_op jit(solution)/shard_map/all_to_all | solution.py:217
  535.8 36.0 %all-to-all-start.4 = ((f32[128,4,4,128]{3,2,1,0:T(4,128)}), f32[128,4,4,128]{3,2,1,0:T(4,128)S(1)}, u32[]{:S(2)}, u32[]{:S(2)}) async-start(f32[128,4,4,128]{3,2,1,0:T(4,128)} %copy.142), calls=%async_computation.4 | async-start | bytes 2097152 | tf_op jit(solution)/shard_map/all_to_all | solution.py:170
  552.6 24.3 %copy-start.10 = (bf16[4,128,4,128]{3,2,1,0:T(4,128)(2,1)S(1)}, bf16[4,128,4,128]{3,2,1,0:T(4,128)(2,1)}, u32[]{:S(2)}) copy-start(bf16[4,128,4,128]{3,2,1,0:T(4,128)(2,1)} %copy-done.9) | copy-start | bytes 1572868
  575.4 1.9 copy-start.18
  575.4 3.5 copy-start.16
  577.3 2.9 copy-start.6
  584.2 7.9 %copy-start.5 = (f32[512,512]{1,0:T(8,128)S(1)}, f32[512,512]{1,0:T(8,128)}, u32[]{:S(2)}) copy-start(f32[512,512]{1,0:T(8,128)} %reshape.210) | copy-start | bytes 3145732
  586.8 5.2 copy-start.7
  586.8 6.8 %copy-start.19 = (f32[512,4]{1,0:T(8,128)S(1)}, f32[512,4]{1,0:T(8,128)}, u32[]{:S(2)}) copy-start(f32[512,4]{1,0:T(8,128)} %copy.139) | copy-start | bytes 24580
  589.4 4.8 copy-start.20
  589.4 5.4 copy-start.8
Sparse Core Ops, SparseCore 0:
  121.0 161.9 all-gather.1
